TPU v7x, 256 devices: a whole 4x4x8 slice. The times are simulated.
256 devices in a mesh: prime: 8 (over z), row: 32 (over x, y, core).
Axes of the slice: x: 4, y: 4, z: 8, core: 2. Of those that a mesh axis runs over, the one named last changes fastest.
Arguments:
- tile_data: bfloat16 [8, 128, 17, 128, 128], P('prime', 'row'), may hold values from -0.125 to 0.125
- tile_slots: int32 [8, 128, 17], P('prime', 'row'), may hold values from 0 to 67, as said below
- requests: int32 [8, 32, 32, 2], P('prime'), may hold values from 0 to 3, as said below
- start_panel: bfloat16 [8, 16384, 128], P('prime', 'row'), may hold values from -6 to 6
- projectors: bfloat16 [8, 16384, 128], P('prime', 'row'), may hold values from -0.09375 to 0.09375
- combine_weights: float32 [8, 8], replicated, may hold values from -2 to 2
Outputs:
- projections_mixed: float32 [8, 6, 128, 128], P(None, None, 'row', 'prime')
- final_panel: bfloat16 [8, 16384, 128], P('prime', 'row')
Inputs may be any that keep to these rules, and one draw needn't show every extreme that they name: `tile_slots`: for each system and each device of row, the last slot of each of its 4 block rows is 64 plus the row's index among them, and the other slots of its rows together name each of 0 to 63 exactly once. `requests`: for each system, taking device and source device, the 2 entries are different.
All inputs are finite; a program needn't handle non-finite values.
Results may differ from a plain program's by a relative error of at most 0.02.
Values may be sent and summed in bfloat16 or wider, within the bound.
A program may use at most 64 MiB of HBM per device.

v0:
```python
import jax
import jax.numpy as jnp
from jax import lax
from jax.sharding import PartitionSpec as P

ITERS = 6


def select_blocks(blocks, positions):
    return blocks[positions]


def shards(tile_data, tile_slots, requests, start_panel, projectors, combine_weights):
    rank_count = lax.axis_size("row")
    my_index = lax.axis_index("row")
    local_primes, local_blocks, stored_tiles, tile_rows, tile_cols = tile_data.shape
    vec_width = start_panel.shape[2]
    fetched = requests.shape[3]
    exchanged = rank_count * fetched
    pick_rows = jax.vmap(select_blocks)
    own_wants = lax.dynamic_index_in_dim(requests, my_index, 1, keepdims=False)
    flat_wants = own_wants.reshape(local_primes, exchanged)
    inside = jnp.clip(tile_slots, 0, exchanged - 1).reshape(local_primes, -1)
    picked = jnp.take_along_axis(flat_wants, inside, axis=1).reshape(tile_slots.shape)
    columns = jnp.where(
        tile_slots < exchanged,
        tile_slots // fetched * local_blocks + picked,
        my_index * local_blocks + tile_slots - exchanged,
    )
    current_panel = start_panel
    projections = []
    for iteration in range(ITERS):
        partial_sum = jnp.einsum(
            "prw,prv->pwv", projectors, current_panel, preferred_element_type=jnp.float32
        )
        projections.append(
            lax.psum_scatter(
                partial_sum.astype(jnp.bfloat16), "row", scatter_dimension=1, tiled=True
            ).astype(jnp.float32)
        )
        gathered = lax.all_gather(current_panel, "row", axis=1, tiled=True)
        gathered = gathered.reshape(local_primes, rank_count * local_blocks, tile_rows, vec_width)
        needed_blocks = pick_rows(gathered, columns)
        product = jnp.einsum(
            "pikab,pikbw->piaw", tile_data, needed_blocks, preferred_element_type=jnp.float32
        )
        current_panel = product.astype(jnp.bfloat16).reshape(
            local_primes, local_blocks * tile_rows, vec_width
        )
    stacked = jnp.stack(projections, axis=1)
    regrouped = lax.all_to_all(stacked, "prime", split_axis=3, concat_axis=0, tiled=True)
    combined = jnp.einsum(
        "qp,pkab->qkab", combine_weights, regrouped, precision=lax.Precision.HIGHEST
    )
    return (combined, current_panel)


def solution(mesh):
    return jax.shard_map(
        shards,
        mesh=mesh,
        in_specs=(
            P("prime", "row", None, None, None),
            P("prime", "row", None),
            P("prime", None, None, None),
            P("prime", "row", None),
            P("prime", "row", None),
            P(),
        ),
        out_specs=(P(None, None, "row", "prime"), P("prime", "row", None)),
        check_vma=False,
    )
```

profile of v0, /device:TPU:1, one launch (start us, length us, event | category | flops | bytes accessed | tf_op | source)
XLA Modules:
  0.0 486.8 jit_solution(9364935634181028703)
XLA Ops:
  9.6 1.2 gather_fusion
  11.8 54.1 %all-gather.7.cloned.1.call-done = bf16[1,16384,128]{2,1,0:T(8,128)(2,1)} async-done(((bf16[1,512,128]{2,1,0:T(8,128)(2,1)}), bf16[1,16384,128]{2,1,0:T(8,128)(2,1)}) %all-gather.7.cloned.1.call-update) | async-done | bytes 4194320 | tf_op jit(solution)/shard_map/all_gather | solution.py:41
  65.9 4.7 gather_fusion.1
  70.6 3.0 fusion.30
  73.7 50.6 %all-gather.9.cloned.1.call-done = bf16[1,16384,128]{2,1,0:T(8,128)(2,1)} async-done(((bf16[1,512,128]{2,1,0:T(8,128)(2,1)}), bf16[1,16384,128]{2,1,0:T(8,128)(2,1)}) %all-gather.9.cloned.1.call-update) | async-done | bytes 4194320 | tf_op jit(solution)/shard_map/all_gather | solution.py:41
  124.3 4.7 gather_fusion.2
  129.0 3.0 fusion.33
  132.1 50.6 %all-gather.11.cloned.1.call-done = bf16[1,16384,128]{2,1,0:T(8,128)(2,1)} async-done(((bf16[1,512,128]{2,1,0:T(8,128)(2,1)}), bf16[1,16384,128]{2,1,0:T(8,128)(2,1)}) %all-gather.11.cloned.1.call-update) | async-done | bytes 4194320 | tf_op jit(solution)/shard_map/all_gather | solution.py:41
  182.8 4.7 gather_fusion.3
  187.4 3.0 fusion.36
  190.5 50.6 %all-gather.13.cloned.1.call-done = bf16[1,16384,128]{2,1,0:T(8,128)(2,1)} async-done(((bf16[1,512,128]{2,1,0:T(8,128)(2,1)}), bf16[1,16384,128]{2,1,0:T(8,128)(2,1)}) %all-gather.13.cloned.1.call-update) | async-done | bytes 4194320 | tf_op jit(solution)/shard_map/all_gather | solution.py:41
  241.2 4.7 gather_fusion.4
  245.9 3.1 fusion.39
  249.0 0.8 fusion.48
  252.7 1.1 fusion.52
  254.6 45.0 %all-gather.15.cloned.1.call-done = bf16[1,16384,128]{2,1,0:T(8,128)(2,1)} async-done(((bf16[1,512,128]{2,1,0:T(8,128)(2,1)}), bf16[1,16384,128]{2,1,0:T(8,128)(2,1)}) %all-gather.15.cloned.1.call-update) | async-done | bytes 4194320 | tf_op jit(solution)/shard_map/all_gather | solution.py:41
  299.6 4.7 gather_fusion.5
  304.3 2.4 fusion.42
  307.0 0.7 copy.36
  309.8 108.3 %all-reduce.9.cloned.1.call-done = (bf16[1,128,128]{2,1,0:T(8,128)(2,1)}, bf16[1,128,128]{2,1,0:T(8,128)(2,1)}, bf16[1,128,128]{2,1,0:T(8,128)(2,1)}, bf16[1,128...) async-done(((bf16[1,128,128]{2,1,0:T(8,128)(2,1)}, bf16[1,128,128]{2,1,0:T(8,128)(2,1)}, bf16[1,128,128]{2,1,0:T(8,128)(2,1)}, ...) | async-done | bytes 196624
  422.6 13.1 %all_to_all.18 = f32[8,1,384]{2,1,0:T(1,128)S(1)} all-to-all(f32[8,1,384]{2,1,0:T(1,128)S(1)} %reshape.336), channel_id=1, replica_groups=mesh['prime'=8,'row'=32] {'prime'}, dimensions={0} | all-to-all | bytes 24576 | tf_op jit(solution)/shard_map/all_to_all | solution.py:51
  438.5 33.7 %all-gather.17.cloned.1.call-done = bf16[1,16384,128]{2,1,0:T(8,128)(2,1)} async-done(((bf16[1,512,128]{2,1,0:T(8,128)(2,1)}), bf16[1,16384,128]{2,1,0:T(8,128)(2,1)}) %all-gather.17.cloned.1.call-update) | async-done | bytes 4194320 | tf_op jit(solution)/shard_map/all_gather | solution.py:41
  472.2 4.7 gather_fusion.6
  476.9 3.0 fusion.45
  (67 shorter events, 16.0 us)
Async XLA Ops:
  7.2 63.5 %copy-start = (bf16[1,4,17,128,128]{4,3,2,1,0:T(8,128)(2,1)S(1)}, bf16[1,4,17,128,128]{4,3,2,1,0:T(8,128)(2,1)}, u32[]{:S(2)}) copy-start(bf16[1,4,17,128,128]{4,3,2,1,0:T(8,128)(2,1)} %param.6) | copy-start | bytes 6684676
  7.2 58.7 %all-gather.7.cloned.1.call-start = ((), (), s32[]{:S(2)}) async-start(), calls=%async_computation.1 | async-start | bytes 4325376 | tf_op jit(solution)/shard_map/all_gather | solution.py:41
  7.9 116.4 %all-gather.9.cloned.1.call-start = ((), (), s32[]{:S(2)}) async-start(), calls=%async_computation.2 | async-start | bytes 4325376 | tf_op jit(solution)/shard_map/all_gather | solution.py:41
  73.7 109.1 %all-gather.11.cloned.1.call-start = ((), (), s32[]{:S(2)}) async-start(), calls=%async_computation.3 | async-start | bytes 4325376 | tf_op jit(solution)/shard_map/all_gather | solution.py:41
  132.1 109.1 %all-gather.13.cloned.1.call-start = ((), (), s32[]{:S(2)}) async-start(), calls=%async_computation.4 | async-start | bytes 4325376 | tf_op jit(solution)/shard_map/all_gather | solution.py:41
  190.5 109.2 %all-gather.15.cloned.1.call-start = ((), (), s32[]{:S(2)}) async-start(), calls=%async_computation.5 | async-start | bytes 4325376 | tf_op jit(solution)/shard_map/all_gather | solution.py:41
  245.8 3.2 copy-start.1
  245.8 3.2 copy-start.6
  245.8 4.1 copy-start.3
  245.8 5.0 %copy-start.4 = (bf16[4,128,128]{1,2,0:T(8,128)(2,1)S(1)}, bf16[4,128,128]{1,2,0:T(8,128)(2,1)}, u32[]{:S(2)}) copy-start(bf16[4,128,128]{1,2,0:T(8,128)(2,1)} %fusion.33) | copy-start | bytes 393220
  245.8 6.0 %copy-start.5 = (bf16[4,128,128]{1,2,0:T(8,128)(2,1)S(1)}, bf16[4,128,128]{1,2,0:T(8,128)(2,1)}, u32[]{:S(2)}) copy-start(bf16[4,128,128]{1,2,0:T(8,128)(2,1)} %fusion.36) | copy-start | bytes 393220
  249.0 169.1 %all-reduce.9.cloned.1.call-start = ((), (), s32[]{:S(2)}) async-start(), calls=%async_computation.7 | async-start | bytes 393216
  304.3 4.2 copy-start.8
  304.3 133.3 %copy-start.7 = (f32[8,8]{1,0:T(8,128)S(1)}, f32[8,8]{1,0:T(8,128)}, u32[]{:S(2)}) copy-start(f32[8,8]{1,0:T(8,128)} %param.11) | copy-start | bytes 772
  306.7 1.1 copy-start.2
  307.7 164.5 %all-gather.17.cloned.1.call-start = ((), (), s32[]{:S(2)}) async-start(), calls=%async_computation.6 | async-start | bytes 4325376 | tf_op jit(solution)/shard_map/all_gather | solution.py:41
Sparse Core Ops, SparseCore 0:
  10.6 55.2 all-gather.6
  73.8 50.5 all-gather.8
  132.2 50.5 all-gather.10
  190.6 50.5 all-gather.12
  249.1 50.5 all-gather.14
  307.9 110.1 all-reduce.8
  421.5 50.6 all-gather.16
where the time goes:
time: 488 us; the launch traced here: 487 us
  waiting for transfers between devices  394 us (81%)
  local copies, waits for them, and re-layouts  41.2 us (8%)
  matrix products  20.6 us (4%)
  between operations  14.9 us (3%)
  blocking collectives  13.1 us (3%)
    all_gather x6, waiting for transfers between devices, shards(): gathered = lax.all_gather(current_panel, 'row', axis=1, tiled=True)  285 us
    unnamed x8, waiting for transfers between devices  110 us
    gather x8, local copies, waits for them, and re-layouts, select_blocks(): return blocks[positions]  28.3 us
    dot_general x6, matrix products, shards(): jnp.einsum('pikab,pikbw->piaw', tile_data, needed_blocks, preferred_eleme...  17.5 us
    all_to_all x1, blocking collectives, shards(): lax.all_to_all(stacked, 'prime', split_axis=3, concat_axis=0, tiled=True)  13.1 us
  transfers between devices with their start and end apart: 7, of which 7 were waited for; matrix products, arithmetic and copies ran while one was open for 4% of the time, Pallas kernels for 0%

commit v1 on v0

--- a/solution.py
+++ b/solution.py
@@ -38,7 +38,9 @@
                 partial_sum.astype(jnp.bfloat16), "row", scatter_dimension=1, tiled=True
             ).astype(jnp.float32)
         )
-        gathered = lax.all_gather(current_panel, "row", axis=1, tiled=True)
+        gathered = jnp.concatenate(
+            lax.all_to_all(jnp.stack([current_panel] * lax.axis_size("row")), "row", 0, 0), axis=1
+        )
         gathered = gathered.reshape(local_primes, rank_count * local_blocks, tile_rows, vec_width)
         needed_blocks = pick_rows(gathered, columns)
         product = jnp.einsum(

time: 488 us -> 548 us (1.12)
  blocking collectives: 13.1 us -> 180 us
  waiting for transfers between devices: 394 us -> 259 us
  starting transfers between devices: 0.29 us -> 20.8 us
  local copies, waits for them, and re-layouts: 41.2 us -> 53.7 us
    all_gather x6 -> x0, waiting for transfers between devices: 285 us -> none  [shards(): gathered = lax.all_gather(current_panel, 'row', axis=1, tiled=True)]
    all_to_all x0 -> x3, blocking collectives: none -> 167 us  [shards(): lax.all_to_all(jnp.stack([current_panel] * lax.axis_size('row')), 'row',...]
    all_to_all x0 -> x3, waiting for transfers between devices: none -> 147 us  [shards(): lax.all_to_all(jnp.stack([current_panel] * lax.axis_size('row')), 'row',...]
    all_to_all x0 -> x3, starting transfers between devices: none -> 20.5 us  [shards(): lax.all_to_all(jnp.stack([current_panel] * lax.axis_size('row')), 'row',...]
    another operation x0 -> x6, local copies, waits for them, and re-layouts: none -> 12.6 us  [shards(): jnp.stack([current_panel] * lax.axis_size('row'))]
    unnamed x8 -> x2, waiting for transfers between devices: 110 us -> 112 us
  transfers between devices with their start and end apart: 7 -> 4, of which waited for: 7 -> 4; matrix products, arithmetic and copies ran while one was open for 4% -> 2% of each run, Pallas kernels for 0% -> 0%
where the time goes in v1:
time: 548 us; the launch traced here: 546 us
  waiting for transfers between devices  259 us (47%)
  blocking collectives  180 us (33%)
  local copies, waits for them, and re-layouts  53.7 us (10%)
  starting transfers between devices  20.8 us (4%)
  matrix products  17 us (3%)
  between operations  15 us (3%)
    all_to_all x3, blocking collectives, shards(): lax.all_to_all(jnp.stack([current_panel] * lax.axis_size('row')), 'row',...  167 us
    all_to_all x3, waiting for transfers between devices, shards(): lax.all_to_all(jnp.stack([current_panel] * lax.axis_size('row')), 'row',...  147 us
    unnamed x2, waiting for transfers between devices  112 us
    gather x8, local copies, waits for them, and re-layouts, select_blocks(): return blocks[positions]  28.3 us
    all_to_all x3, starting transfers between devices, shards(): lax.all_to_all(jnp.stack([current_panel] * lax.axis_size('row')), 'row',...  20.5 us
    dot_general x6, matrix products, shards(): jnp.einsum('pikab,pikbw->piaw', tile_data, needed_blocks, preferred_eleme...  14.8 us
    all_to_all x1, blocking collectives, shards(): lax.all_to_all(stacked, 'prime', split_axis=3, concat_axis=0, tiled=True)  13.1 us
    another operation x6, local copies, waits for them, and re-layouts, shards(): jnp.stack([current_panel] * lax.axis_size('row'))  12.6 us
  transfers between devices with their start and end apart: 4, of which 4 were waited for; matrix products, arithmetic and copies ran while one was open for 2% of the time, Pallas kernels for 0%

profile of v1, /device:TPU:1, one launch (start us, length us, event | category | flops | bytes accessed | tf_op | source)
XLA Modules:
  0.0 545.8 jit_solution(7073562340643803525)
XLA Ops:
  7.2 4.0 stack.36
  11.1 8.8 %all-to-all-start = ((bf16[32,1,512,128]{3,2,1,0:T(8,128)(2,1)}), bf16[32,1,512,128]{3,2,1,0:T(8,128)(2,1)}, u32[]{:S(2)}, u32[]{:S(2)}) async-start(bf16[32,1,512,128]{3,2,1,0:T(8,128)(2,1)} %stack.36), calls=%async_computation | async-start | bytes 8388608 | tf_op jit(solution)/shard_map/all_to_all | solution.py:42
  22.4 49.8 %all-to-all-done = bf16[32,1,512,128]{3,2,1,0:T(8,128)(2,1)} async-done(((bf16[32,1,512,128]{3,2,1,0:T(8,128)(2,1)}), bf16[32,1,512,128]{3,2,1,0:T(8,128)(2,1)}, u32[]{:S(2)}, u32[]{:S(2)}) %all-to-all-start) | async-done | bytes 4194336 | tf_op jit(solution)/shard_map/all_to_all | solution.py:42
  72.1 4.7 gather_fusion.1
  76.8 2.4 fusion.30
  80.2 57.6 %all_to_all.48 = bf16[32,1,512,128]{3,2,1,0:T(8,128)(2,1)} all-to-all(bf16[32,1,512,128]{3,2,1,0:T(8,128)(2,1)S(1)} %stack.38), channel_id=1, replica_groups=mesh['prime'=8,'row'=32] {'row'}, dimensions={0} | all-to-all | bytes 8388608 | tf_op jit(solution)/shard_map/all_to_all | solution.py:42
  137.8 4.7 gather_fusion.2
  145.8 54.5 %all_to_all.49 = bf16[32,1,512,128]{3,2,1,0:T(8,128)(2,1)} all-to-all(bf16[32,1,512,128]{3,2,1,0:T(8,128)(2,1)S(1)} %stack.40), channel_id=1, replica_groups=mesh['prime'=8,'row'=32] {'row'}, dimensions={0} | all-to-all | bytes 8388608 | tf_op jit(solution)/shard_map/all_to_all | solution.py:42
  200.3 4.7 gather_fusion.3
  205.0 2.4 fusion.36
  208.3 54.5 %all_to_all.50 = bf16[32,1,512,128]{3,2,1,0:T(8,128)(2,1)} all-to-all(bf16[32,1,512,128]{3,2,1,0:T(8,128)(2,1)S(1)} %stack.42), channel_id=1, replica_groups=mesh['prime'=8,'row'=32] {'row'}, dimensions={0} | all-to-all | bytes 8388608 | tf_op jit(solution)/shard_map/all_to_all | solution.py:42
  262.8 4.7 gather_fusion.4
  269.8 2.9 stack.44
  272.7 4.8 all-to-all-start.4
  282.4 47.3 %all-to-all-done.4 = bf16[32,1,512,128]{3,2,1,0:T(8,128)(2,1)} async-done(((bf16[32,1,512,128]{3,2,1,0:T(8,128)(2,1)}), bf16[32,1,512,128]{3,2,1,0:T(8,128)(2,1)}, u32[]{:S(2)}, u32[]{:S(2)}) %all-to-all-start.4) | async-done | bytes 4194336 | tf_op jit(solution)/shard_map/all_to_all | solution.py:42
  329.7 4.7 gather_fusion.5
  334.4 2.4 fusion.42
  339.1 112.2 %all-reduce.9.cloned.1.call-done = (bf16[1,128,128]{2,1,0:T(8,128)(2,1)}, bf16[1,128,128]{2,1,0:T(8,128)(2,1)}, bf16[1,128,128]{2,1,0:T(8,128)(2,1)}, bf16[1,128...) async-done(((bf16[1,128,128]{2,1,0:T(8,128)(2,1)}, bf16[1,128,128]{2,1,0:T(8,128)(2,1)}, bf16[1,128,128]{2,1,0:T(8,128)(2,1)}, ...) | async-done | bytes 196624
  455.9 13.1 %all_to_all.51 = f32[8,1,384]{2,1,0:T(1,128)S(1)} all-to-all(f32[8,1,384]{2,1,0:T(1,128)S(1)} %reshape.325), channel_id=1, replica_groups=mesh['prime'=8,'row'=32] {'prime'}, dimensions={0} | all-to-all | bytes 24576 | tf_op jit(solution)/shard_map/all_to_all | solution.py:53
  469.0 2.9 stack.93
  472.0 7.0 %all-to-all-start.6 = ((bf16[32,1,512,128]{3,2,1,0:T(8,128)(2,1)}), bf16[32,1,512,128]{3,2,1,0:T(8,128)(2,1)}, u32[]{:S(2)}, u32[]{:S(2)}) async-start(bf16[32,1,512,128]{3,2,1,0:T(8,128)(2,1)} %stack.93), calls=%async_computation.6 | async-start | bytes 8388608 | tf_op jit(solution)/shard_map/all_to_all | solution.py:42
  481.7 49.5 %all-to-all-done.6 = bf16[32,1,512,128]{3,2,1,0:T(8,128)(2,1)} async-done(((bf16[32,1,512,128]{3,2,1,0:T(8,128)(2,1)}), bf16[32,1,512,128]{3,2,1,0:T(8,128)(2,1)}, u32[]{:S(2)}, u32[]{:S(2)}) %all-to-all-start.6) | async-done | bytes 4194336 | tf_op jit(solution)/shard_map/all_to_all | solution.py:42
  531.2 4.7 gather_fusion.6
  535.9 3.0 fusion.45
  (58 shorter events, 23.6 us)
Async XLA Ops:
  7.2 69.7 %copy-start = (bf16[1,4,17,128,128]{4,3,2,1,0:T(8,128)(2,1)S(1)}, bf16[1,4,17,128,128]{4,3,2,1,0:T(8,128)(2,1)}, u32[]{:S(2)}) copy-start(bf16[1,4,17,128,128]{4,3,2,1,0:T(8,128)(2,1)} %param.6) | copy-start | bytes 6684676
  11.1 9.7 %copy-start.3 = (s32[1,4,17]{2,1,0:T(4,128)S(1)}, s32[1,4,17]{2,1,0:T(4,128)}, u32[]{:S(2)}) copy-start(s32[1,4,17]{2,1,0:T(4,128)} %param.7) | copy-start | bytes 820
  11.1 61.0 %all-to-all-start = ((bf16[32,1,512,128]{3,2,1,0:T(8,128)(2,1)}), bf16[32,1,512,128]{3,2,1,0:T(8,128)(2,1)}, u32[]{:S(2)}, u32[]{:S(2)}) async-start(bf16[32,1,512,128]{3,2,1,0:T(8,128)(2,1)} %stack.36), calls=%async_computation | async-start | bytes 8388608 | tf_op jit(solution)/shard_map/all_to_all | solution.py:42
  272.7 5.0 copy-start.1
  272.7 5.0 copy-start.2
  272.7 57.0 %all-to-all-start.4 = ((bf16[32,1,512,128]{3,2,1,0:T(8,128)(2,1)}), bf16[32,1,512,128]{3,2,1,0:T(8,128)(2,1)}, u32[]{:S(2)}, u32[]{:S(2)}) async-start(bf16[32,1,512,128]{3,2,1,0:T(8,128)(2,1)} %stack.44), calls=%async_computation.4 | async-start | bytes 8388608 | tf_op jit(solution)/shard_map/all_to_all | solution.py:42
  277.5 173.8 %all-reduce.9.cloned.1.call-start = ((), (), s32[]{:S(2)}) async-start(), calls=%async_computation.7 | async-start | bytes 393216
  334.4 3.4 copy-start.5
  472.0 8.8 %copy-start.4 = (f32[8,8]{1,0:T(8,128)S(1)}, f32[8,8]{1,0:T(8,128)}, u32[]{:S(2)}) copy-start(f32[8,8]{1,0:T(8,128)} %param.11) | copy-start | bytes 772
  472.0 59.3 %all-to-all-start.6 = ((bf16[32,1,512,128]{3,2,1,0:T(8,128)(2,1)}), bf16[32,1,512,128]{3,2,1,0:T(8,128)(2,1)}, u32[]{:S(2)}, u32[]{:S(2)}) async-start(bf16[32,1,512,128]{3,2,1,0:T(8,128)(2,1)} %stack.93), calls=%async_computation.6 | async-start | bytes 8388608 | tf_op jit(solution)/shard_map/all_to_all | solution.py:42
Sparse Core Ops, SparseCore 0:
  337.9 113.4 all-reduce.8
